TPU v7x, 32 devices: a whole 2x2x4 slice. The times are simulated.
32 devices in a mesh: dp: 8 (over z, y), group: 4 (over x, core).
Axes of the slice: x: 2, y: 2, z: 4, core: 2. Of those that a mesh axis runs over, the one named last changes fastest.
Arguments:
- gradients: float32 [32, 3, 320, 960], P(('dp', 'group')), may hold values from -0.8 to 0.8
- errors: bfloat16 [32, 3, 320, 960], P(('dp', 'group')), may hold values from -0.59765625 to 0.59765625
- q_init: float32 [3, 960, 32], replicated, may hold values from -0.1875 to 0.1875
- owners: int32 [3], replicated, may hold values from 0 to 31, as said below
- buckets: int32 [3], replicated, may hold values from 0 to 3
- learn_rates: float32 [4], replicated, may hold values from 0.2 to 1
- beta_values: float32 [4], replicated, may hold values from 0.5 to 0.95
- momentum: bfloat16 [64, 320, 960], P(('dp', 'group')), may hold values from -3 to 3
Outputs:
- new_errors: bfloat16 [32, 3, 320, 960], P(('dp', 'group'))
- weight_steps: bfloat16 [32, 3, 320, 960], P(('dp', 'group'))
- new_momentum: bfloat16 [64, 320, 960], P(('dp', 'group'))
Inputs may be any that keep to these rules, and one draw needn't show every extreme that they name: `owners`: no device owns more than 2 matrices, and some device owns exactly 2.
All inputs are finite; a program needn't handle non-finite values.
Results may differ from a plain program's by a relative error of at most 0.001.
Values may be sent and summed in bfloat16 or wider, within the bound.
No kernel may reach another device: no remote copies, remote signals or barrier semaphores. Data moves between devices by JAX's collectives and lax.ppermute only.
A program may use at most 64 MiB of HBM per device.

v0:
```python
import jax
import jax.numpy as jnp
from jax import lax
from jax.sharding import PartitionSpec as P


def from_root(value, axis, source):
    kept = jnp.where(lax.axis_index(axis) == source, value, 0).astype(value.dtype)
    return lax.psum(kept, axis)


def on_device(gradients, errors, q_init, owners, buckets, learn_rates, beta_values, momentum):
    highest = lax.Precision.HIGHEST
    slot_count = momentum.shape[0]
    mat_count = owners.shape[0]
    bucket_count = learn_rates.shape[0]
    my_index = lax.axis_index(("dp", "group"))
    positions = jnp.arange(mat_count, dtype=jnp.int32)
    earlier = (owners[None, :] == owners[:, None]) & (positions[None, :] < positions[:, None])
    slot_list = jnp.sum(earlier.astype(jnp.int32), axis=1)
    bucket_hits = buckets[:, None] == jnp.arange(bucket_count, dtype=jnp.int32)[None, :]
    rate_list = jnp.sum(jnp.where(bucket_hits, learn_rates[None, :], 0.0), axis=1)
    beta_list = jnp.sum(jnp.where(bucket_hits, beta_values[None, :], 0.0), axis=1)
    merged = gradients[0] + errors[0].astype(jnp.float32)
    p_local = jnp.einsum("mkd,mdr->mkr", merged, q_init, precision=highest)
    p_sum = lax.psum(p_local, ("dp", "group"))
    gram_matrix = jnp.einsum("mkr,mks->mrs", p_sum, p_sum, precision=highest)
    lower_factor = jnp.linalg.cholesky(gram_matrix)
    p_hat = lax.linalg.triangular_solve(
        lower_factor, p_sum, left_side=False, lower=True, transpose_a=True
    )
    q_local = jnp.einsum("mkd,mkr->mdr", merged, p_hat, precision=highest)
    q_sum = lax.psum(q_local, ("dp", "group"))
    approx = jnp.einsum("mkr,mdr->mkd", p_hat, q_local, precision=highest)
    new_errors = (merged - approx).astype(jnp.bfloat16)
    update = jnp.einsum("mkr,mdr->mkd", p_hat, q_sum, precision=highest)
    slot_range = jnp.arange(slot_count, dtype=jnp.int32)
    new_slab = jnp.zeros(momentum.shape, jnp.float32)
    step_list = []
    for matrix in range(mat_count):
        old_state = lax.dynamic_index_in_dim(momentum, slot_list[matrix], 0, keepdims=False).astype(
            jnp.float32
        )
        mom_new = beta_list[matrix] * old_state + update[matrix]
        step_value = (-rate_list[matrix] * (update[matrix] + beta_list[matrix] * mom_new)).astype(
            jnp.bfloat16
        )
        step_value = from_root(step_value, ("dp", "group"), owners[matrix])
        step_list.append(step_value)
        selected = (slot_range == slot_list[matrix]) & (owners[matrix] == my_index)
        new_slab = new_slab + jnp.where(selected[:, None, None], mom_new[None], 0.0)
    return (new_errors[None], jnp.stack(step_list)[None], new_slab.astype(jnp.bfloat16))


def solution(mesh):
    placed = (
        P(("dp", "group"), None, None, None),
        P(("dp", "group"), None, None, None),
        P(),
        P(),
        P(),
        P(),
        P(),
        P(("dp", "group"), None, None),
    )
    return jax.shard_map(
        on_device,
        mesh=mesh,
        in_specs=placed,
        out_specs=(
            P(("dp", "group"), None, None, None),
            P(("dp", "group"), None, None, None),
            P(("dp", "group"), None, None),
        ),
        check_vma=False,
    )
```

profile of v0, /device:TPU:0, one launch (start us, length us, event | category | flops | bytes accessed | tf_op | source)
XLA Modules:
  0.0 456.5 jit_solution(16836187007871859211)
XLA Ops:
  7.2 0.0 copy-start
  7.2 0.0 copy-start.5
  7.2 0.0 all-reduce.5.cloned.1.call-start
  7.2 0.9 copy-done
  8.2 7.3 %fusion.2 = f32[3,320,32]{1,2,0:T(8,128)} fusion(f32[3,960,32]{1,2,0:T(8,128)S(1)} %copy-done, f32[1,3,320,960]{3,2,1,0:T(8,128)} %param.8, bf16[1,3,320,960]{3,2,1,0:T(8,128)(2,1)} %param.9), kind=kOutput, calls=%fused_computation.3 | convolution fusion | flops 355737600 | bytes 6021120 | tf_op jit(solution)/shard_map/mkd,mdr->mkr/dot_general | solution.py:25
  15.5 0.0 all-reduce.5.cloned.1.call-update
  15.5 0.0 copy-done.5
  15.5 0.2 convert_reduce_fusion
  15.7 0.7 fusion.28
  20.2 0.6 fusion.29
  24.7 114.3 %all-reduce.5.cloned.1.call-done = f32[3,320,32]{1,2,0:T(8,128)} async-done(((f32[3,320,32]{1,2,0:T(8,128)}), f32[3,320,32]{1,2,0:T(8,128)}) %all-reduce.5.cloned.1.call-update) | async-done | bytes 122896 | tf_op jit(solution)/shard_map/psum | solution.py:26
  139.0 1.3 fusion.32
  140.3 0.1 copy.13
  140.4 8.8 %custom-call.7 = f32[3,32,32]{2,1,0:T(8,128)S(1)} custom-call(f32[3,32,32]{2,1,0:T(8,128)S(1)} %fusion.26), custom_call_target="Cholesky" | custom-call | tf_op jit(solution)/shard_map/jit(cholesky)/cholesky | solution.py:28
  149.2 0.1 compare_reduce_fusion
  149.3 0.1 select_bitcast_fusion
  149.4 7.4 %custom-call.8 = f32[3,1,32,32]{2,3,1,0:T(8,128)S(1)} custom-call(f32[3,1,32,32]{3,2,1,0:T(8,128)S(1)} %select_bitcast_fusion), custom_call_target="InvertDiagBlocksLowerTriangular" | custom-call | tf_op jit(solution)/shard_map/triangular_solve | solution.py:29
  156.8 1.3 fusion.24
  158.0 0.0 copy-done.2
  158.1 4.8 %fusion = f32[3,960,32]{1,2,0:T(8,128)S(1)} fusion(f32[3,320,32]{1,2,0:T(8,128)S(1)} %fusion.24, f32[1,3,320,960]{3,2,1,0:T(8,128)} %param.8, bf16[1,3,320,960]{3,2,1,0:T(8,128)(2,1)S(1)} %copy-done.2), kind=kOutput, calls=%fused_computation.1 | convolution fusion | flops 355737600 | bytes 6021120 | tf_op jit(solution)/shard_map/mkd,mkr->mdr/dot_general | solution.py:32
  162.9 0.0 copy-start.4
  162.9 0.0 copy-start.6
  162.9 0.0 copy-start.7
  162.9 0.0 copy-start.8
  162.9 6.3 %fusion.5 = bf16[1,3,320,960]{3,2,1,0:T(8,128)(2,1)} fusion(f32[3,320,32]{1,2,0:T(8,128)S(1)} %fusion.24, f32[3,960,32]{1,2,0:T(8,128)S(1)} %fusion, f32[1,3,320,960]{3,2,1,0:T(8,128)} %param.8, bf16[1,3,320,960]{3,2,1,0:T(8,128)(2,1)S(1)} %copy-done.2), kind=kOutput, calls=%fused_computation.9 | convolution fusion | flops 357580800 | bytes 7864320 | tf_op jit(solution)/shard_map/mkr,mdr->mkd/dot_general | solution.py:34
  169.2 0.0 copy-done.4
  169.2 0.0 all-reduce.7.cloned.1.call-start
  169.3 0.7 all-reduce.7.cloned.1.call-update
  170.0 0.2 all-reduce.9.cloned.1.call-start
  170.2 0.0 copy-done.6
  170.2 0.0 copy-done.7
  170.2 0.0 copy-done.8
  170.2 0.2 select_reduce_fusion.2
  170.4 0.7 fusion.30
  174.9 0.0 copy-start.3
  174.9 130.5 %all-reduce.7.cloned.1.call-done = f32[3,960,32]{1,2,0:T(8,128)} async-done(((f32[3,960,32]{1,2,0:T(8,128)}), f32[3,960,32]{1,2,0:T(8,128)}) %all-reduce.7.cloned.1.call-update) | async-done | bytes 368656 | tf_op jit(solution)/shard_map/psum | solution.py:33
  305.4 4.3 fusion.33
  309.7 0.0 copy-start.1
  309.7 0.0 copy-done.3
  309.7 3.9 fusion.19
  313.6 0.0 copy-done.1
  313.6 0.0 all-reduce.9.cloned.1.call-update
  313.6 0.6 compare_and_fusion.2
  314.2 1.3 compare_and_fusion
  315.5 4.8 %add_bitcast_fusion.2 = (f32[320,960]{1,0:T(8,128)S(1)}, f32[320,960]{1,0:T(8,128)S(1)}, f32[320,960]{1,0:T(8,128)S(1)}) fusion(f32[3,320,960]{2,1,0:T(8,128)} %copy-done.1, f32[]{:T(128)} %bitcast.8, bf16[2,320,960]{2,1,0:T(8,128)(2,1)S(1)} %copy-done.3, s32[]{:T(128)S(6)} %select_n.55, s32[]{:T(128)S(6)} %select_n.58, f32[]{:T(128)} %bitcast.15, ...), kind=kLoop, calls=%fused_computation.27 | loop fusion | flops 2764800 | bytes 9216024 | tf_op jit(solution)/shard_map/jit(_where)/broadcast_in_dim | solution.py:51
  320.4 1.7 add_convert_fusion
  322.1 125.0 %all-reduce.9.cloned.1.call-done = (bf16[1,320,960]{2,1,0:T(8,128)(2,1)}, bf16[1,320,960]{2,1,0:T(8,128)(2,1)}, bf16[1,320,960]{2,1,0:T(8,128)(2,1)}) async-done(((bf16[1,320,960]{2,1,0:T(8,128)(2,1)}, bf16[1,320,960]{2,1,0:T(8,128)(2,1)}, bf16[1,320,960]{2,1,0:T(8,128)(2,1)}), (bf16[1,320,960]{2,1,0:T(8,128)(2,1)}, bf16[1,320,960]{2,1,0:T(8,128)(2,1)}, ...) | async-done | bytes 1843216 | tf_op jit(solution)/shard_map/psum | solution.py:9
  447.0 3.0 maximum_bitcast_fusion
  (5 shorter events, 0.1 us)
Async XLA Ops:
  7.2 1.0 copy-start
  7.2 8.3 %copy-start.5 = (s32[3]{0:T(128)S(1)}, s32[3]{0:T(128)}, u32[]{:S(2)}) copy-start(s32[3]{0:T(128)} %param.11) | copy-start | bytes 40
  7.2 131.8 %all-reduce.5.cloned.1.call-start = ((), (), s32[]{:S(2)}) async-start(), calls=%async_computation | async-start | bytes 294912 | tf_op jit(solution)/shard_map/psum | solution.py:26
  8.2 149.9 %copy-start.2 = (bf16[1,3,320,960]{3,2,1,0:T(8,128)(2,1)S(1)}, bf16[1,3,320,960]{3,2,1,0:T(8,128)(2,1)}, u32[]{:S(2)}) copy-start(bf16[1,3,320,960]{3,2,1,0:T(8,128)(2,1)} %param.9) | copy-start | bytes 5529604
  162.9 6.4 %copy-start.4 = (f32[3,960,32]{1,2,0:T(8,128)}, f32[3,960,32]{1,2,0:T(8,128)S(1)}, u32[]{:S(2)}) copy-start(f32[3,960,32]{1,2,0:T(8,128)S(1)} %fusion) | copy-start | bytes 1105924
  162.9 7.3 %copy-start.6 = (f32[4]{0:T(128)S(1)}, f32[4]{0:T(128)}, u32[]{:S(2)}) copy-start(f32[4]{0:T(128)} %param.13) | copy-start | bytes 52
  162.9 7.3 %copy-start.7 = (s32[3]{0:T(128)S(1)}, s32[3]{0:T(128)}, u32[]{:S(2)}) copy-start(s32[3]{0:T(128)} %param.12) | copy-start | bytes 40
  162.9 7.3 %copy-start.8 = (f32[4]{0:T(128)S(1)}, f32[4]{0:T(128)}, u32[]{:S(2)}) copy-start(f32[4]{0:T(128)} %param.14) | copy-start | bytes 52
  169.2 136.1 %all-reduce.7.cloned.1.call-start = ((), (), s32[]{:S(2)}) async-start(), calls=%async_computation.1 | async-start | bytes 786432 | tf_op jit(solution)/shard_map/psum | solution.py:33
  170.0 277.0 %all-reduce.9.cloned.1.call-start = ((), (), s32[]{:S(2)}) async-start(), calls=%async_computation.2 | async-start | bytes 3932160 | tf_op jit(solution)/shard_map/psum | solution.py:9
  174.9 134.8 %copy-start.3 = (bf16[2,320,960]{2,1,0:T(8,128)(2,1)S(1)}, bf16[2,320,960]{2,1,0:T(8,128)(2,1)}, u32[]{:S(2)}) copy-start(bf16[2,320,960]{2,1,0:T(8,128)(2,1)} %param.15) | copy-start | bytes 3686404
  309.7 3.9 copy-start.1
Sparse Core Ops, SparseCore 0:
  15.6 123.3 all-reduce.4
  175.9 129.3 all-reduce.6
  313.7 133.2 all-reduce.8
where the time goes:
time: 457 us
  waiting for transfers between devices  371 us (81%)
  other arithmetic  32.1 us (7%)
  between operations  25.4 us (6%)
  matrix products  25.2 us (6%)
    psum x1, waiting for transfers between devices, on_device(): q_sum = lax.psum(q_local, ('dp', 'group'))  131 us
    psum x1, waiting for transfers between devices, from_root(): return lax.psum(kept, axis)  125 us
    psum x1, waiting for transfers between devices, on_device(): p_sum = lax.psum(p_local, ('dp', 'group'))  114 us
  transfers between devices with their start and end apart: 3, of which 3 were waited for; matrix products, arithmetic and copies ran while one was open for 2% of the time, Pallas kernels for 0%

commit v1 on v0

--- a/solution.py
+++ b/solution.py
@@ -30,7 +30,7 @@
         lower_factor, p_sum, left_side=False, lower=True, transpose_a=True
     )
     q_local = jnp.einsum("mkd,mkr->mdr", merged, p_hat, precision=highest)
-    q_sum = lax.psum(q_local, ("dp", "group"))
+    q_sum = lax.psum(lax.psum(q_local, "group"), "dp")
     approx = jnp.einsum("mkr,mdr->mkd", p_hat, q_local, precision=highest)
     new_errors = (merged - approx).astype(jnp.bfloat16)
     update = jnp.einsum("mkr,mdr->mkd", p_hat, q_sum, precision=highest)

time: 457 us -> 434 us (0.950)
  waiting for transfers between devices: 371 us -> 348 us
    psum x1 -> x2, waiting for transfers between devices: 131 us -> 98.5 us  [on_device(): q_sum = lax.psum(lax.psum(q_local, 'group'), 'dp')]
    psum x1, waiting for transfers between devices: 114 us -> 123 us  [on_device(): p_sum = lax.psum(p_local, ('dp', 'group'))]
  transfers between devices with their start and end apart: 3 -> 4, of which waited for: 3 -> 4; matrix products, arithmetic and copies ran while one was open for 2% -> 2% of each run, Pallas kernels for 0% -> 0%
where the time goes in v1:
time: 434 us
  waiting for transfers between devices  348 us (80%)
  other arithmetic  32.1 us (7%)
  between operations  25.5 us (6%)
  matrix products  25.2 us (6%)
    psum x1, waiting for transfers between devices, from_root(): return lax.psum(kept, axis)  125 us
    psum x1, waiting for transfers between devices, on_device(): p_sum = lax.psum(p_local, ('dp', 'group'))  123 us
    psum x2, waiting for transfers between devices, on_device(): q_sum = lax.psum(lax.psum(q_local, 'group'), 'dp')  98.5 us
    another operation x4, other arithmetic, on_device(): lower_factor = jnp.linalg.cholesky(gram_matrix)  8.96 us
  transfers between devices with their start and end apart: 4, of which 4 were waited for; matrix products, arithmetic and copies ran while one was open for 2% of the time, Pallas kernels for 0%

profile of v1, /device:TPU:0, one launch (start us, length us, event | category | flops | bytes accessed | tf_op | source)
XLA Modules:
  0.0 433.9 jit_solution(11584485724202148600)
XLA Ops:
  7.2 0.0 copy-start
  7.2 0.0 all-reduce.6.cloned.1.call-start
  7.2 0.9 copy-done
  8.2 7.3 %fusion.2 = f32[3,320,32]{1,2,0:T(8,128)} fusion(f32[3,960,32]{1,2,0:T(8,128)S(1)} %copy-done, f32[1,3,320,960]{3,2,1,0:T(8,128)} %param.8, bf16[1,3,320,960]{3,2,1,0:T(8,128)(2,1)} %param.9), kind=kOutput, calls=%fused_computation.3 | convolution fusion | flops 355737600 | bytes 6021120 | tf_op jit(solution)/shard_map/mkd,mdr->mkr/dot_general | solution.py:25
  15.5 0.0 all-reduce.6.cloned.1.call-update
  15.5 123.5 %all-reduce.6.cloned.1.call-done = f32[3,320,32]{1,2,0:T(8,128)} async-done(((f32[3,320,32]{1,2,0:T(8,128)}), f32[3,320,32]{1,2,0:T(8,128)}) %all-reduce.6.cloned.1.call-update) | async-done | bytes 122896 | tf_op jit(solution)/shard_map/psum | solution.py:26
  139.0 1.3 fusion.32
  140.3 0.1 copy.13
  140.4 8.8 %custom-call.7 = f32[3,32,32]{2,1,0:T(8,128)S(1)} custom-call(f32[3,32,32]{2,1,0:T(8,128)S(1)} %fusion.26), custom_call_target="Cholesky" | custom-call | tf_op jit(solution)/shard_map/jit(cholesky)/cholesky | solution.py:28
  149.2 0.1 compare_reduce_fusion
  149.3 0.1 select_bitcast_fusion
  149.4 7.4 %custom-call.8 = f32[3,1,32,32]{2,3,1,0:T(8,128)S(1)} custom-call(f32[3,1,32,32]{3,2,1,0:T(8,128)S(1)} %select_bitcast_fusion), custom_call_target="InvertDiagBlocksLowerTriangular" | custom-call | tf_op jit(solution)/shard_map/triangular_solve | solution.py:29
  156.8 1.3 fusion.24
  158.0 0.0 copy-done.2
  158.1 4.8 %fusion = f32[3,960,32]{1,2,0:T(8,128)S(1)} fusion(f32[3,320,32]{1,2,0:T(8,128)S(1)} %fusion.24, f32[1,3,320,960]{3,2,1,0:T(8,128)} %param.8, bf16[1,3,320,960]{3,2,1,0:T(8,128)(2,1)S(1)} %copy-done.2), kind=kOutput, calls=%fused_computation.1 | convolution fusion | flops 355737600 | bytes 6021120 | tf_op jit(solution)/shard_map/mkd,mkr->mdr/dot_general | solution.py:32
  162.9 0.0 copy-start.4
  162.9 0.0 copy-start.5
  162.9 0.0 copy-start.6
  162.9 0.0 copy-start.7
  162.9 0.0 copy-start.8
  162.9 6.3 %fusion.5 = bf16[1,3,320,960]{3,2,1,0:T(8,128)(2,1)} fusion(f32[3,320,32]{1,2,0:T(8,128)S(1)} %fusion.24, f32[3,960,32]{1,2,0:T(8,128)S(1)} %fusion, f32[1,3,320,960]{3,2,1,0:T(8,128)} %param.8, bf16[1,3,320,960]{3,2,1,0:T(8,128)(2,1)S(1)} %copy-done.2), kind=kOutput, calls=%fused_computation.9 | convolution fusion | flops 357580800 | bytes 7864320 | tf_op jit(solution)/shard_map/mkr,mdr->mkd/dot_general | solution.py:34
  169.3 0.0 copy-done.4
  169.3 0.0 all-reduce.8.cloned.1.call-start
  169.3 0.7 all-reduce.8.cloned.1.call-update
  170.0 0.0 all-reduce.10.cloned.1.call-start
  170.0 0.0 copy-done.5
  170.1 0.2 convert_reduce_fusion
  170.2 37.4 %all-reduce.8.cloned.1.call-done = f32[3,960,32]{1,2,0:T(8,128)} async-done(((f32[3,960,32]{1,2,0:T(8,128)}), f32[3,960,32]{1,2,0:T(8,128)}) %all-reduce.8.cloned.1.call-update) | async-done | bytes 368656 | tf_op jit(solution)/shard_map/psum | solution.py:33
  207.6 0.0 all-reduce.10.cloned.1.call-update
  207.6 0.2 all-reduce.12.cloned.1.call-start
  207.8 0.7 fusion.28
  212.3 0.6 fusion.29
  216.8 0.0 copy-done.6
  216.8 0.0 copy-done.7
  216.8 0.0 copy-done.8
  216.9 0.2 select_reduce_fusion.2
  217.0 0.7 fusion.30
  221.5 0.0 copy-start.3
  221.6 61.2 %all-reduce.10.cloned.1.call-done = f32[3,960,32]{1,2,0:T(8,128)} async-done(((f32[3,960,32]{1,2,0:T(8,128)}), f32[3,960,32]{1,2,0:T(8,128)}) %all-reduce.10.cloned.1.call-update) | async-done | bytes 368656 | tf_op jit(solution)/shard_map/psum | solution.py:33
  282.7 4.3 fusion.33
  287.0 3.9 fusion.19
  290.9 0.0 all-reduce.12.cloned.1.call-update
  290.9 0.6 compare_and_fusion.2
  291.6 1.3 compare_and_fusion
  292.9 4.8 %add_bitcast_fusion.2 = (f32[320,960]{1,0:T(8,128)S(1)}, f32[320,960]{1,0:T(8,128)S(1)}, f32[320,960]{1,0:T(8,128)S(1)}) fusion(f32[3,320,960]{2,1,0:T(8,128)} %copy-done.1, f32[]{:T(128)} %bitcast.8, bf16[2,320,960]{2,1,0:T(8,128)(2,1)S(1)} %copy-done.3, s32[]{:T(128)S(6)} %select_n.55, s32[]{:T(128)S(6)} %select_n.58, f32[]{:T(128)} %bitcast.15, ...), kind=kLoop, calls=%fused_computation.27 | loop fusion | flops 2764800 | bytes 9216024 | tf_op jit(solution)/shard_map/jit(_where)/broadcast_in_dim | solution.py:51
  297.7 1.7 add_convert_fusion
  299.4 125.0 %all-reduce.12.cloned.1.call-done = (bf16[1,320,960]{2,1,0:T(8,128)(2,1)}, bf16[1,320,960]{2,1,0:T(8,128)(2,1)}, bf16[1,320,960]{2,1,0:T(8,128)(2,1)}) async-done(((bf16[1,320,960]{2,1,0:T(8,128)(2,1)}, bf16[1,320,960]{2,1,0:T(8,128)(2,1)}, bf16[1,320,960]{2,1,0:T(8,128)(2,1)}), (bf16[1,320,960]{2,1,0:T(8,128)(2,1)}, bf16[1,320,960]{2,1,0:T(8,128)(2,1)}, ...) | async-done | bytes 1843216 | tf_op jit(solution)/shard_map/psum | solution.py:9
  424.4 3.0 maximum_bitcast_fusion
  (8 shorter events, 0.1 us)
Async XLA Ops:
  7.2 1.0 copy-start
  7.2 131.8 %all-reduce.6.cloned.1.call-start = ((), (), s32[]{:S(2)}) async-start(), calls=%async_computation | async-start | bytes 294912 | tf_op jit(solution)/shard_map/psum | solution.py:26
  8.2 149.9 %copy-start.2 = (bf16[1,3,320,960]{3,2,1,0:T(8,128)(2,1)S(1)}, bf16[1,3,320,960]{3,2,1,0:T(8,128)(2,1)}, u32[]{:S(2)}) copy-start(bf16[1,3,320,960]{3,2,1,0:T(8,128)(2,1)} %param.9) | copy-start | bytes 5529604
  162.9 6.4 %copy-start.4 = (f32[3,960,32]{1,2,0:T(8,128)}, f32[3,960,32]{1,2,0:T(8,128)S(1)}, u32[]{:S(2)}) copy-start(f32[3,960,32]{1,2,0:T(8,128)S(1)} %fusion) | copy-start | bytes 1105924
  162.9 7.2 %copy-start.5 = (s32[3]{0:T(128)S(1)}, s32[3]{0:T(128)}, u32[]{:S(2)}) copy-start(s32[3]{0:T(128)} %param.11) | copy-start | bytes 40
  162.9 53.9 %copy-start.6 = (f32[4]{0:T(128)S(1)}, f32[4]{0:T(128)}, u32[]{:S(2)}) copy-start(f32[4]{0:T(128)} %param.13) | copy-start | bytes 52
  162.9 53.9 %copy-start.7 = (s32[3]{0:T(128)S(1)}, s32[3]{0:T(128)}, u32[]{:S(2)}) copy-start(s32[3]{0:T(128)} %param.12) | copy-start | bytes 40
  162.9 53.9 %copy-start.8 = (f32[4]{0:T(128)S(1)}, f32[4]{0:T(128)}, u32[]{:S(2)}) copy-start(f32[4]{0:T(128)} %param.14) | copy-start | bytes 52
  169.3 38.3 %all-reduce.8.cloned.1.call-start = ((), (), s32[]{:S(2)}) async-start(), calls=%async_computation.1 | async-start | bytes 786432 | tf_op jit(solution)/shard_map/psum | solution.py:33
  170.0 112.7 %all-reduce.10.cloned.1.call-start = ((), (), s32[]{:S(2)}) async-start(), calls=%async_computation.2 | async-start | bytes 786432 | tf_op jit(solution)/shard_map/psum | solution.py:33
  207.6 216.8 %all-reduce.12.cloned.1.call-start = ((), (), s32[]{:S(2)}) async-start(), calls=%async_computation.3 | async-start | bytes 3932160 | tf_op jit(solution)/shard_map/psum | solution.py:9
  221.5 65.5 %copy-start.3 = (bf16[2,320,960]{2,1,0:T(8,128)(2,1)S(1)}, bf16[2,320,960]{2,1,0:T(8,128)(2,1)}, u32[]{:S(2)}) copy-start(bf16[2,320,960]{2,1,0:T(8,128)(2,1)} %param.15) | copy-start | bytes 3686404
  287.0 3.9 copy-start.1
Sparse Core Ops, SparseCore 0:
  15.6 123.3 all-reduce.5
  173.0 34.5 all-reduce.7
  211.3 71.3 all-reduce.9
  291.1 133.3 all-reduce.11
